TPU v7x, 32 devices: a whole 2x2x4 slice. The times are simulated.
32 devices in a mesh: dp: 8 (over z, x), tensor: 4 (over y, core).
Axes of the slice: x: 2, y: 2, z: 4, core: 2. Of those that a mesh axis runs over, the one named last changes fastest.
Arguments:
- tokens: bfloat16 [8192, 2048], P('dp'), may hold values from -6 to 6
- lengths: int32 [8], P('dp'), may hold values from 1 to 1024, 4915 in all
- norm_attn: float32 [2048], P('dp'), may hold values from 0.5 to 1.5
- query_proj: float32 [2048, 1024], P('dp', 'tensor'), may hold values from -0.125 to 0.125
- key_proj: float32 [2048, 1024], P('dp', 'tensor'), may hold values from -0.125 to 0.125
- value_proj: float32 [2048, 2048], P('dp', 'tensor'), may hold values from -0.125 to 0.125
- outgate_proj: float32 [2048, 2048], P('dp', 'tensor'), may hold values from -0.125 to 0.125
- rank_proj: float32 [2048, 16], P('dp'), may hold values from -0.125 to 0.125
- decay_proj: float32 [16, 4, 256], P(None, 'tensor', 'dp'), may hold values from -1.5 to 1.5
- decay_bias: float32 [4, 256], P('tensor', 'dp'), may hold values from -4 to 5
- head_gain: float32 [512], P('dp'), may hold values from 0.5 to 1.5
- out_proj: float32 [2048, 2048], P('tensor', 'dp'), may hold values from -0.25 to 0.25
- norm_ffn: float32 [2048], P('dp'), may hold values from 0.5 to 1.5
- gate_proj: float32 [2048, 5632], P('dp', 'tensor'), may hold values from -0.125 to 0.125
- up_proj: float32 [2048, 5632], P('dp', 'tensor'), may hold values from -0.125 to 0.125
- down_proj: float32 [5632, 2048], P('tensor', 'dp'), may hold values from -0.15625 to 0.15625
- cotangent: bfloat16 [8192, 2048], P('dp'), may hold values from -6 to 6
Outputs:
- output: bfloat16 [8192, 2048], P('dp')
- grad_tokens: bfloat16 [8192, 2048], P('dp')
- grad_norm_attn: float32 [2048], P('dp')
- grad_query_proj: float32 [2048, 1024], P('dp', 'tensor')
- grad_key_proj: float32 [2048, 1024], P('dp', 'tensor')
- grad_value_proj: float32 [2048, 2048], P('dp', 'tensor')
- grad_outgate_proj: float32 [2048, 2048], P('dp', 'tensor')
- grad_rank_proj: float32 [2048, 16], P('dp')
- grad_decay_proj: float32 [16, 4, 256], P(None, 'tensor', 'dp')
- grad_decay_bias: float32 [4, 256], P('tensor', 'dp')
- grad_head_gain: float32 [512], P('dp')
- grad_out_proj: float32 [2048, 2048], P('tensor', 'dp')
- grad_norm_ffn: float32 [2048], P('dp')
- grad_gate_proj: float32 [2048, 5632], P('dp', 'tensor')
- grad_up_proj: float32 [2048, 5632], P('dp', 'tensor')
- grad_down_proj: float32 [5632, 2048], P('tensor', 'dp')
Inputs may be any that keep to these rules, and one draw needn't show every extreme that they name: `lengths`: each slot's live positions come first; some slot is full.
All inputs are finite; a program needn't handle non-finite values. No bound on the sum of `lengths` on one device may be relied on, other than what follows from the above.
Results may differ from a plain program's by a relative error of at most 0.04.
Values may be sent and summed in bfloat16 or wider, within the bound.
A program may use at most 256 MiB of HBM per device.

v0:
```python
import jax
import jax.numpy as jnp
from jax import lax
from jax.sharding import PartitionSpec as P

DK = 256
DV = 512
GROUP = 64
SEQ_LEN = 1024
norm_eps = 1e-06
head_eps = 1.0
highest_precision = lax.Precision.HIGHEST


def rms_scale(values, gain):
    return values * lax.rsqrt(jnp.mean(values * values, axis=-1, keepdims=True) + norm_eps) * gain


def project(left, right):
    return jnp.dot(left, right, preferred_element_type=jnp.float32)


def collect(left, right):
    return lax.dot_general(
        left, right, (((0,), (0,)), ((), ())), preferred_element_type=jnp.float32
    )


def against(left, right):
    return lax.dot_general(
        left, right, (((1,), (1,)), ((), ())), preferred_element_type=jnp.float32
    )


def group_step(running_state, block):
    query_matrix, key_matrix, value_matrix, decay = block
    cumulative_decay = jnp.cumsum(decay, axis=1)
    steps = decay.shape[1]
    lower = (jnp.arange(steps)[:, None] >= jnp.arange(steps)[None, :]).astype(jnp.float32)
    spread = (
        jnp.exp(jnp.minimum(cumulative_decay[:, :, None, :] - cumulative_decay[:, None, :, :], 0.0))
        * lower[None, :, :, None]
    )
    weighted = query_matrix[:, :, None, :] * spread
    scores = jnp.einsum("hijk,hjk->hij", weighted, key_matrix, precision=highest_precision)
    inner = jnp.einsum("hij,hjv->hiv", scores, value_matrix, precision=highest_precision)
    outer_product = jnp.einsum(
        "muq,mqj->muj",
        query_matrix * jnp.exp(cumulative_decay),
        running_state,
        precision=highest_precision,
    )
    final_decay_row = cumulative_decay[:, -1:, :]
    carried_state = jnp.exp(final_decay_row[:, 0, :])[:, :, None] * running_state
    carried_state = carried_state + jnp.einsum(
        "zbm,zbi->zmi",
        key_matrix * jnp.exp(final_decay_row - cumulative_decay),
        value_matrix,
        precision=highest_precision,
    )
    return (carried_state, inner + outer_product)


def recurrence(query_matrix, key_matrix, value_matrix, decay):
    length = query_matrix.shape[0]
    heads = query_matrix.shape[1]
    count = length // GROUP

    def split(values):
        return jnp.transpose(values.reshape(count, GROUP, heads, values.shape[2]), (0, 2, 1, 3))

    start = jnp.zeros((heads, key_matrix.shape[2], value_matrix.shape[2]), jnp.float32)
    _, blocks = lax.scan(
        jax.checkpoint(group_step),
        start,
        (split(query_matrix), split(key_matrix), split(value_matrix), split(decay)),
    )
    return jnp.transpose(blocks, (0, 2, 1, 3)).reshape(length, heads, value_matrix.shape[2])


def mixer(
    query_matrix,
    key_matrix,
    value_matrix,
    outgate_rows,
    rank_rows,
    decay_weight,
    bias_weight,
    gain_weight,
):
    heads = bias_weight.shape[0]
    length = query_matrix.shape[0]
    seqs = length // SEQ_LEN
    before = jnp.dot(
        rank_rows,
        decay_weight.reshape(decay_weight.shape[0], -1),
        precision=highest_precision,
        preferred_element_type=jnp.float32,
    ) + bias_weight.reshape(-1)
    decay = jax.nn.log_sigmoid(before) / 16.0

    def arrange(values, width):
        return values.reshape(seqs, SEQ_LEN, heads, width)

    scale = DK ** (-0.5)
    mixed = jax.vmap(recurrence)(
        arrange(query_matrix * scale, DK),
        arrange(key_matrix, DK),
        arrange(value_matrix, DV),
        arrange(decay, DK),
    )
    mixed = mixed.reshape(length, heads, DV)
    normed = (
        mixed * lax.rsqrt(jnp.mean(mixed * mixed, axis=-1, keepdims=True) + head_eps) * gain_weight
    )
    return (normed * jax.nn.silu(outgate_rows.reshape(length, heads, DV))).reshape(
        length, heads * DV
    )


def swiglu(gate_rows, up_rows):
    return jax.nn.silu(gate_rows) * up_rows


def local(
    tokens,
    lengths,
    norm_attn,
    query_proj,
    key_proj,
    value_proj,
    outgate_proj,
    rank_proj,
    decay_proj,
    decay_bias,
    head_gain,
    out_proj,
    norm_ffn,
    gate_proj,
    up_proj,
    down_proj,
    cotangent,
):
    half = jnp.bfloat16
    (
        gain_attn,
        query_full,
        key_full,
        value_full,
        outgate_full,
        rank_full,
        decay_full,
        bias_full,
        head_full,
        out_full,
    ) = (
        lax.all_gather(norm_attn.astype(half), "dp", axis=0, tiled=True),
        lax.all_gather(query_proj.astype(half), "dp", axis=0, tiled=True),
        lax.all_gather(key_proj.astype(half), "dp", axis=0, tiled=True),
        lax.all_gather(value_proj.astype(half), "dp", axis=0, tiled=True),
        lax.all_gather(outgate_proj.astype(half), "dp", axis=0, tiled=True),
        lax.all_gather(rank_proj.astype(half), "dp", axis=0, tiled=True),
        lax.all_gather(decay_proj.astype(half), "dp", axis=2, tiled=True),
        lax.all_gather(decay_bias.astype(half), "dp", axis=1, tiled=True),
        lax.all_gather(head_gain.astype(half), "dp", axis=0, tiled=True),
        lax.all_gather(out_proj.astype(half), "dp", axis=1, tiled=True),
    )
    rows_total = tokens.shape[0]
    positions = jnp.arange(SEQ_LEN, dtype=jnp.int32)
    mask = (positions[None, :] < lengths[:, None]).astype(jnp.float32).reshape(rows_total, 1)
    tokens_full = tokens.astype(jnp.float32)
    normed, pull_first = jax.vjp(rms_scale, tokens_full, gain_attn.astype(jnp.float32))
    normed_half = normed.astype(half)
    query_matrix = project(normed_half, query_full)
    key_matrix = project(normed_half, key_full)
    value_matrix = project(normed_half, value_full)
    outgate_rows = project(normed_half, outgate_full)
    rank_rows = project(normed_half, rank_full)
    gated, pull_mix = jax.vjp(
        mixer,
        query_matrix,
        key_matrix,
        value_matrix,
        outgate_rows,
        rank_rows,
        decay_full.astype(jnp.float32),
        bias_full.astype(jnp.float32),
        head_full.astype(jnp.float32),
    )
    gated_half = gated.astype(half)
    attn = lax.psum(project(gated_half, out_full), "tensor")
    middle = tokens_full + attn
    gain_ffn, gate_full, up_full, down_full = (
        lax.all_gather(norm_ffn.astype(half), "dp", axis=0, tiled=True),
        lax.all_gather(gate_proj.astype(half), "dp", axis=0, tiled=True),
        lax.all_gather(up_proj.astype(half), "dp", axis=0, tiled=True),
        lax.all_gather(down_proj.astype(half), "dp", axis=1, tiled=True),
    )
    normed_ffn, pull_second = jax.vjp(rms_scale, middle, gain_ffn.astype(jnp.float32))
    normed_ffn_half = normed_ffn.astype(half)
    gate_rows = project(normed_ffn_half, gate_full)
    up_rows = project(normed_ffn_half, up_full)
    hidden, pull_glu = jax.vjp(swiglu, gate_rows, up_rows)
    hidden_half = hidden.astype(half)
    ffn = lax.psum(project(hidden_half, down_full).astype(jnp.bfloat16), "tensor").astype(
        jnp.float32
    )
    output = (mask * (middle + ffn)).astype(half)
    d_out = cotangent.astype(jnp.float32) * mask
    d_out_half = d_out.astype(half)
    gain_ffn, gate_full, up_full, down_full = (
        lax.all_gather(norm_ffn.astype(half), "dp", axis=0, tiled=True),
        lax.all_gather(gate_proj.astype(half), "dp", axis=0, tiled=True),
        lax.all_gather(up_proj.astype(half), "dp", axis=0, tiled=True),
        lax.all_gather(down_proj.astype(half), "dp", axis=1, tiled=True),
    )
    grad_down = collect(hidden_half, d_out_half)
    d_hidden = against(d_out_half, down_full)
    d_gate, d_up = pull_glu(d_hidden)
    d_gate_half = d_gate.astype(half)
    d_up_half = d_up.astype(half)
    grad_gate = collect(normed_ffn_half, d_gate_half)
    grad_up = collect(normed_ffn_half, d_up_half)
    d_normed_ffn = lax.psum(
        (against(d_gate_half, gate_full) + against(d_up_half, up_full)).astype(jnp.bfloat16),
        "tensor",
    ).astype(jnp.float32)
    d_middle_norm, grad_gain_ffn = pull_second(d_normed_ffn)
    grad_norm_ffn, grad_gate_proj, grad_up_proj, grad_down_proj = (
        lax.psum_scatter(
            grad_gain_ffn.astype(jnp.bfloat16), "dp", scatter_dimension=0, tiled=True
        ).astype(jnp.float32),
        lax.psum_scatter(
            grad_gate.astype(jnp.bfloat16), "dp", scatter_dimension=0, tiled=True
        ).astype(jnp.float32),
        lax.psum_scatter(
            grad_up.astype(jnp.bfloat16), "dp", scatter_dimension=0, tiled=True
        ).astype(jnp.float32),
        lax.psum_scatter(
            grad_down.astype(jnp.bfloat16), "dp", scatter_dimension=1, tiled=True
        ).astype(jnp.float32),
    )
    d_middle = d_out + d_middle_norm
    d_attn_half = d_middle.astype(half)
    (
        gain_attn,
        query_full,
        key_full,
        value_full,
        outgate_full,
        rank_full,
        decay_full,
        bias_full,
        head_full,
        out_full,
    ) = (
        lax.all_gather(norm_attn.astype(half), "dp", axis=0, tiled=True),
        lax.all_gather(query_proj.astype(half), "dp", axis=0, tiled=True),
        lax.all_gather(key_proj.astype(half), "dp", axis=0, tiled=True),
        lax.all_gather(value_proj.astype(half), "dp", axis=0, tiled=True),
        lax.all_gather(outgate_proj.astype(half), "dp", axis=0, tiled=True),
        lax.all_gather(rank_proj.astype(half), "dp", axis=0, tiled=True),
        lax.all_gather(decay_proj.astype(half), "dp", axis=2, tiled=True),
        lax.all_gather(decay_bias.astype(half), "dp", axis=1, tiled=True),
        lax.all_gather(head_gain.astype(half), "dp", axis=0, tiled=True),
        lax.all_gather(out_proj.astype(half), "dp", axis=1, tiled=True),
    )
    grad_out = collect(gated_half, d_attn_half)
    d_gated = against(d_attn_half, out_full)
    d_query, d_key, d_value, d_outgate, d_rank, grad_decay, grad_bias, grad_head = pull_mix(d_gated)
    d_query_half = d_query.astype(half)
    d_key_half = d_key.astype(half)
    d_value_half = d_value.astype(half)
    d_outgate_half = d_outgate.astype(half)
    grad_query = collect(normed_half, d_query_half)
    grad_key = collect(normed_half, d_key_half)
    grad_value = collect(normed_half, d_value_half)
    grad_outgate = collect(normed_half, d_outgate_half)
    d_normed_part = (
        against(d_query_half, query_full)
        + against(d_key_half, key_full)
        + against(d_value_half, value_full)
        + against(d_outgate_half, outgate_full)
    )
    d_normed, d_rank_total, grad_head_total = (
        lax.psum(d_normed_part.astype(jnp.bfloat16), "tensor").astype(jnp.float32),
        lax.psum(d_rank.astype(jnp.bfloat16), "tensor").astype(jnp.float32),
        lax.psum(grad_head.astype(jnp.bfloat16), "tensor").astype(jnp.float32),
    )
    d_rank_half = d_rank_total.astype(half)
    grad_rank = collect(normed_half, d_rank_half)
    d_normed = d_normed + against(d_rank_half, rank_full)
    d_tokens_norm, grad_gain_attn = pull_first(d_normed)
    grad_tokens = (d_middle + d_tokens_norm).astype(half)
    (
        grad_norm_attn,
        grad_query_proj,
        grad_key_proj,
        grad_value_proj,
        grad_outgate_proj,
        grad_rank_proj,
        grad_decay_proj,
        grad_decay_bias,
        grad_head_gain,
        grad_out_proj,
    ) = (
        lax.psum_scatter(
            grad_gain_attn.astype(jnp.bfloat16), "dp", scatter_dimension=0, tiled=True
        ).astype(jnp.float32),
        lax.psum_scatter(
            grad_query.astype(jnp.bfloat16), "dp", scatter_dimension=0, tiled=True
        ).astype(jnp.float32),
        lax.psum_scatter(
            grad_key.astype(jnp.bfloat16), "dp", scatter_dimension=0, tiled=True
        ).astype(jnp.float32),
        lax.psum_scatter(
            grad_value.astype(jnp.bfloat16), "dp", scatter_dimension=0, tiled=True
        ).astype(jnp.float32),
        lax.psum_scatter(
            grad_outgate.astype(jnp.bfloat16), "dp", scatter_dimension=0, tiled=True
        ).astype(jnp.float32),
        lax.psum_scatter(
            grad_rank.astype(jnp.bfloat16), "dp", scatter_dimension=0, tiled=True
        ).astype(jnp.float32),
        lax.psum_scatter(
            grad_decay.astype(jnp.bfloat16), "dp", scatter_dimension=2, tiled=True
        ).astype(jnp.float32),
        lax.psum_scatter(
            grad_bias.astype(jnp.bfloat16), "dp", scatter_dimension=1, tiled=True
        ).astype(jnp.float32),
        lax.psum_scatter(
            grad_head_total.astype(jnp.bfloat16), "dp", scatter_dimension=0, tiled=True
        ).astype(jnp.float32),
        lax.psum_scatter(
            grad_out.astype(jnp.bfloat16), "dp", scatter_dimension=1, tiled=True
        ).astype(jnp.float32),
    )
    return (
        output,
        grad_tokens,
        grad_norm_attn,
        grad_query_proj,
        grad_key_proj,
        grad_value_proj,
        grad_outgate_proj,
        grad_rank_proj,
        grad_decay_proj,
        grad_decay_bias,
        grad_head_gain,
        grad_out_proj,
        grad_norm_ffn,
        grad_gate_proj,
        grad_up_proj,
        grad_down_proj,
    )


def solution(mesh):
    return jax.shard_map(
        local,
        mesh=mesh,
        in_specs=(
            P("dp", None),
            P("dp"),
            P("dp"),
            P("dp", "tensor"),
            P("dp", "tensor"),
            P("dp", "tensor"),
            P("dp", "tensor"),
            P("dp", None),
            P(None, "tensor", "dp"),
            P("tensor", "dp"),
            P("dp"),
            P("tensor", "dp"),
            P("dp"),
            P("dp", "tensor"),
            P("dp", "tensor"),
            P("tensor", "dp"),
            P("dp", None),
        ),
        out_specs=(
            P("dp", None),
            P("dp", None),
            P("dp"),
            P("dp", "tensor"),
            P("dp", "tensor"),
            P("dp", "tensor"),
            P("dp", "tensor"),
            P("dp", None),
            P(None, "tensor", "dp"),
            P("tensor", "dp"),
            P("dp"),
            P("tensor", "dp"),
            P("dp"),
            P("dp", "tensor"),
            P("dp", "tensor"),
            P("tensor", "dp"),
        ),
        check_vma=False,
    )
```

profile of v0, /device:TPU:0, one launch (start us, length us, event | category | flops | bytes accessed | tf_op | source)
XLA Modules:
  0.0 2493.8 jit_solution(15633964255061561891)
XLA Ops:
  19.4 22.3 all-gather
  41.7 30.6 %all_gather.52 = bf16[2048,16]{0,1:T(8,128)(2,1)S(1)} all-gather(bf16[256,16]{0,1:T(8,128)(2,1)S(1)} %convert_element_type.283), channel_id=1, replica_groups=mesh['dp'=8,'tensor'=4] {'dp'}, dimensions={0}, use_global_device_ids=true | all-gather | bytes 73728 | tf_op jit(solution)/shard_map/all_gather | solution.py:162
  74.7 17.5 all-reduce.7
  92.4 30.9 %all_gather.53 = bf16[16,1,256]{0,1,2:T(2,128)(2,1)S(1)} all-gather(bf16[16,1,32]{0,1,2:T(2,128)(2,1)S(1)} %copy.93), channel_id=1, replica_groups=mesh['dp'=8,'tensor'=4] {'dp'}, dimensions={2}, use_global_device_ids=true | all-gather | bytes 9216 | tf_op jit(solution)/shard_map/all_gather | solution.py:163
  153.0 229.3 %while.40 = (s32[]{:T(128)}, f32[1,1,256,512]{3,2,1,0:T(8,128)S(1)}, f32[16,1,1,64,512]{4,3,2,1,0:T(8,128)S(1)}, f32[16,1,1,256,512]{4,3,2,1,0:T(8,128)}, f32[16...) while((s32[]{:T(128)}, ...), condition=%wide.region_3.4_spmd.clone.clone, body=%wide.region_1.3_spmd.clone.sunk.clone | while | flops 245047296 | bytes 12723313 | solution.py:73
  402.8 18.1 all-gather.1
  421.6 127.8 %all-reduce.13.cloned.1.call-done = f32[1024,2048]{1,0:T(8,128)} async-done(((f32[1024,2048]{1,0:T(8,128)}), f32[1024,2048]{1,0:T(8,128)}) %all-reduce.13.cloned.1.call-update) | async-done | bytes 8388624 | tf_op jit(solution)/shard_map/psum | solution.py:191
  561.1 82.9 %all-gather.21.cloned.1.call-done = bf16[2048,1408]{1,0:T(8,128)(2,1)} async-done(((bf16[256,1408]{1,0:T(8,128)(2,1)}), bf16[2048,1408]{1,0:T(8,128)(2,1)}) %all-gather.21.cloned.1.call-update) | async-done | bytes 5767184 | tf_op jit(solution)/shard_map/all_gather | solution.py:195
  656.2 80.5 %all-gather.23.cloned.1.call-done = bf16[2048,1408]{1,0:T(8,128)(2,1)} async-done(((bf16[256,1408]{1,0:T(8,128)(2,1)}), bf16[2048,1408]{1,0:T(8,128)(2,1)}) %all-gather.23.cloned.1.call-update) | async-done | bytes 5767184 | tf_op jit(solution)/shard_map/all_gather | solution.py:196
  748.4 81.7 %all-gather.25.cloned.1.call-done = bf16[1408,2048]{1,0:T(8,128)(2,1)} async-done(((bf16[1408,256]{1,0:T(8,128)(2,1)}), bf16[1408,2048]{1,0:T(8,128)(2,1)}) %all-gather.25.cloned.1.call-update) | async-done | bytes 5767184 | tf_op jit(solution)/shard_map/all_gather | solution.py:197
  867.1 81.9 %all-reduce.15.cloned.1.call-done = bf16[1024,2048]{1,0:T(8,128)(2,1)} async-done(((bf16[1024,2048]{1,0:T(8,128)(2,1)}), bf16[1024,2048]{1,0:T(8,128)(2,1)}) %all-reduce.15.cloned.1.call-update) | async-done | bytes 4194320 | tf_op jit(solution)/shard_map/psum | solution.py:224
  969.6 466.3 %while.41 = (s32[]{:T(128)}, f32[1,1,256,512]{2,3,1,0:T(8,128)S(1)}, f32[16,1,1,64,256]{4,3,2,1,0:T(8,128)S(1)}, bf16[16,1,1,64,256]{4,3,2,1,0:T(8,128)(2,1)}, b...) while((s32[]{:T(128)}, ...), condition=%wide.region_19.20_spmd.clone.clone, body=%wide.region_11.19_spmd.clone.sunk.clone | while | flops 502210560 | bytes 24297648 | solution.py:73
  1559.2 23.8 reduce-scatter.34.cloned.1.call-done
  1584.4 56.2 %reduce-scatter.24.cloned.1.call-done = bf16[256,16]{0,1:T(8,128)(2,1)} async-done(((bf16[2048,16]{0,1:T(8,128)(2,1)}), bf16[256,16]{0,1:T(8,128)(2,1)}) %reduce-scatter.24.cloned.1.call-update) | async-done | bytes 8208 | tf_op jit(solution)/shard_map/reduce_scatter | solution.py:322
  1641.8 65.8 %reduce-scatter.16.cloned.1.call-done = bf16[256,256]{1,0:T(8,128)(2,1)} async-done(((bf16[2048,256]{1,0:T(8,128)(2,1)}), bf16[256,256]{1,0:T(8,128)(2,1)}) %reduce-scatter.16.cloned.1.call-update) | async-done | bytes 131088 | tf_op jit(solution)/shard_map/reduce_scatter | solution.py:310
  1709.2 65.5 %reduce-scatter.18.cloned.1.call-done = bf16[256,256]{1,0:T(8,128)(2,1)} async-done(((bf16[2048,256]{1,0:T(8,128)(2,1)}), bf16[256,256]{1,0:T(8,128)(2,1)}) %reduce-scatter.18.cloned.1.call-update) | async-done | bytes 131088 | tf_op jit(solution)/shard_map/reduce_scatter | solution.py:313
  1776.3 152.7 %all-reduce.17.cloned.1.call-done = (bf16[1024,2048]{1,0:T(8,128)(2,1)}, bf16[1024,2048]{1,0:T(8,128)(2,1)}) async-done(((bf16[1024,2048]{1,0:T(8,128)(2,1)}, bf16[1024,2048]{1,0:T(8,128)(2,1)}), (bf16[1024,2048]{1,0:T(8,128)(2,1)}, bf16[1024,2048]{1,0:T(8,128)(2,1)})) %all-reduce.17.cloned.1.call-update) | async-done | bytes 8388624 | tf_op jit(solution)/shard_map/psum | solution.py:205
  1936.4 22.3 all-reduce.6
  1965.2 36.4 %reduce-scatter.26.cloned.1.call-done = bf16[512,256]{1,0:T(8,128)(2,1)} async-done(((bf16[512,2048]{1,0:T(8,128)(2,1)}), bf16[512,256]{1,0:T(8,128)(2,1)}) %reduce-scatter.26.cloned.1.call-update) | async-done | bytes 262160 | tf_op jit(solution)/shard_map/reduce_scatter | solution.py:334
  2003.4 69.1 %reduce-scatter.20.cloned.1.call-done = bf16[256,512]{1,0:T(8,128)(2,1)} async-done(((bf16[2048,512]{1,0:T(8,128)(2,1)}), bf16[256,512]{1,0:T(8,128)(2,1)}) %reduce-scatter.20.cloned.1.call-update) | async-done | bytes 262160 | tf_op jit(solution)/shard_map/reduce_scatter | solution.py:316
  2074.2 69.1 %reduce-scatter.22.cloned.1.call-done = bf16[256,512]{1,0:T(8,128)(2,1)} async-done(((bf16[2048,512]{1,0:T(8,128)(2,1)}), bf16[256,512]{1,0:T(8,128)(2,1)}) %reduce-scatter.22.cloned.1.call-update) | async-done | bytes 262160 | tf_op jit(solution)/shard_map/reduce_scatter | solution.py:319
  2161.6 94.9 %reduce-scatter.28.cloned.1.call-done = bf16[256,1408]{1,0:T(8,128)(2,1)} async-done(((bf16[2048,1408]{1,0:T(8,128)(2,1)}), bf16[256,1408]{1,0:T(8,128)(2,1)}) %reduce-scatter.28.cloned.1.call-update) | async-done | bytes 720912 | tf_op jit(solution)/shard_map/reduce_scatter | solution.py:233
  2258.8 111.3 %reduce-scatter.30.cloned.1.call-done = bf16[256,1408]{1,0:T(8,128)(2,1)} async-done(((bf16[2048,1408]{1,0:T(8,128)(2,1)}), bf16[256,1408]{1,0:T(8,128)(2,1)}) %reduce-scatter.30.cloned.1.call-update) | async-done | bytes 720912 | tf_op jit(solution)/shard_map/reduce_scatter | solution.py:236
  2372.5 111.8 %reduce-scatter.32.cloned.1.call-done = bf16[1408,256]{1,0:T(8,128)(2,1)} async-done(((bf16[1408,2048]{1,0:T(8,128)(2,1)}), bf16[1408,256]{1,0:T(8,128)(2,1)}) %reduce-scatter.32.cloned.1.call-update) | async-done | bytes 720912 | tf_op jit(solution)/shard_map/reduce_scatter | solution.py:239
  (926 shorter events, 1019.1 us)
Async XLA Ops:
  7.2 125.4 %all-gather.15.cloned.1.call-start = ((), (), s32[]{:S(2)}) async-start(), calls=%async_computation.13 | async-start | bytes 1179648 | tf_op jit(solution)/shard_map/all_gather | solution.py:158
  8.9 128.4 %all-gather.11.cloned.1.call-start = ((), (), s32[]{:S(2)}) async-start(), calls=%async_computation.11 | async-start | bytes 1179648 | tf_op jit(solution)/shard_map/all_gather | solution.py:159
  10.6 135.9 %all-gather.13.cloned.1.call-start = ((), (), s32[]{:S(2)}) async-start(), calls=%async_computation.12 | async-start | bytes 2359296 | tf_op jit(solution)/shard_map/all_gather | solution.py:160
  12.5 370.2 %all-gather.17.cloned.1.call-start = ((), (), s32[]{:S(2)}) async-start(), calls=%async_computation.14 | async-start | bytes 2359296 | tf_op jit(solution)/shard_map/all_gather | solution.py:161
  14.3 375.9 %all-gather.19.cloned.1.call-start = ((), (), s32[]{:S(2)}) async-start(), calls=%async_computation.15 | async-start | bytes 2359296 | tf_op jit(solution)/shard_map/all_gather | solution.py:166
  16.2 533.2 %all-reduce.13.cloned.1.call-start = ((), (), s32[]{:S(2)}) async-start(), calls=%async_computation.16 | async-start | bytes 16777216 | tf_op jit(solution)/shard_map/psum | solution.py:191
  397.8 246.2 %all-gather.21.cloned.1.call-start = ((), (), s32[]{:S(2)}) async-start(), calls=%async_computation.17 | async-start | bytes 6488064 | tf_op jit(solution)/shard_map/all_gather | solution.py:195
  400.1 336.6 %all-gather.23.cloned.1.call-start = ((), (), s32[]{:S(2)}) async-start(), calls=%async_computation.18 | async-start | bytes 6488064 | tf_op jit(solution)/shard_map/all_gather | solution.py:196
  401.2 428.9 %all-gather.25.cloned.1.call-start = ((), (), s32[]{:S(2)}) async-start(), calls=%async_computation.19 | async-start | bytes 6488064 | tf_op jit(solution)/shard_map/all_gather | solution.py:197
  402.7 546.3 %all-reduce.15.cloned.1.call-start = ((), (), s32[]{:S(2)}) async-start(), calls=%async_computation.20 | async-start | bytes 8388608 | tf_op jit(solution)/shard_map/psum | solution.py:224
  865.2 692.7 %reduce-scatter.36.cloned.1.call-start = ((), (), s32[]{:S(2)}) async-start(), calls=%async_computation.31 | async-start | bytes 73728
  1454.6 128.4 %reduce-scatter.34.cloned.1.call-start = ((), (), s32[]{:S(2)}) async-start(), calls=%async_computation.30 | async-start | bytes 73728
  1456.0 184.5 %reduce-scatter.24.cloned.1.call-start = ((), (), s32[]{:S(2)}) async-start(), calls=%async_computation.25 | async-start | bytes 73728 | tf_op jit(solution)/shard_map/reduce_scatter | solution.py:322
  1456.8 250.8 %reduce-scatter.16.cloned.1.call-start = ((), (), s32[]{:S(2)}) async-start(), calls=%async_computation.21 | async-start | bytes 1179648 | tf_op jit(solution)/shard_map/reduce_scatter | solution.py:310
  1461.3 313.4 %reduce-scatter.18.cloned.1.call-start = ((), (), s32[]{:S(2)}) async-start(), calls=%async_computation.22 | async-start | bytes 1179648 | tf_op jit(solution)/shard_map/reduce_scatter | solution.py:313
  1474.8 454.2 %all-reduce.17.cloned.1.call-start = ((), (), s32[]{:S(2)}) async-start(), calls=%async_computation.32 | async-start | bytes 16777216 | tf_op jit(solution)/shard_map/psum | solution.py:205
  1499.2 502.4 %reduce-scatter.26.cloned.1.call-start = ((), (), s32[]{:S(2)}) async-start(), calls=%async_computation.26 | async-start | bytes 2359296 | tf_op jit(solution)/shard_map/reduce_scatter | solution.py:334
  1507.5 564.9 %reduce-scatter.20.cloned.1.call-start = ((), (), s32[]{:S(2)}) async-start(), calls=%async_computation.23 | async-start | bytes 2359296 | tf_op jit(solution)/shard_map/reduce_scatter | solution.py:316
  1513.5 629.9 %reduce-scatter.22.cloned.1.call-start = ((), (), s32[]{:S(2)}) async-start(), calls=%async_computation.24 | async-start | bytes 2359296 | tf_op jit(solution)/shard_map/reduce_scatter | solution.py:319
  1519.7 736.8 %reduce-scatter.28.cloned.1.call-start = ((), (), s32[]{:S(2)}) async-start(), calls=%async_computation.27 | async-start | bytes 6488064 | tf_op jit(solution)/shard_map/reduce_scatter | solution.py:233
  1530.9 839.3 %reduce-scatter.30.cloned.1.call-start = ((), (), s32[]{:S(2)}) async-start(), calls=%async_computation.28 | async-start | bytes 6488064 | tf_op jit(solution)/shard_map/reduce_scatter | solution.py:236
  1543.6 940.7 %reduce-scatter.32.cloned.1.call-start = ((), (), s32[]{:S(2)}) async-start(), calls=%async_computation.29 | async-start | bytes 6488064 | tf_op jit(solution)/shard_map/reduce_scatter | solution.py:239
  1556.5 372.6 %copy-start.25 = (f32[8,1,256]{2,1,0:T(1,128)S(1)}, f32[8,1,256]{2,1,0:T(1,128)}, u32[]{:S(2)}) copy-start(f32[8,1,256]{2,1,0:T(1,128)} %copy-done.24) | copy-start | bytes 24580
  1556.5 372.6 %copy-start.29 = (f32[1024]{0:T(1024)S(1)}, f32[1024]{0:T(1024)}, u32[]{:S(2)}) copy-start(f32[1024]{0:T(1024)} %copy-done.28) | copy-start | bytes 12292
  (45 other events, 1430.8 us)
Sparse Core Ops, SparseCore 0:
  10.7 43.2 all-gather.14
  56.7 38.8 all-gather.10
  98.3 48.2 all-gather.12
  149.1 47.6 all-gather.16
  199.3 49.1 all-gather.18
  397.9 151.4 all-reduce.12
  551.5 92.4 all-gather.20
  646.2 90.4 all-gather.22
  738.7 91.3 all-gather.24
  865.3 83.6 all-reduce.14
  1454.7 62.8 reduce-scatter.35
  1521.5 61.4 reduce-scatter.33
  1586.7 53.8 reduce-scatter.23
  1644.4 63.1 reduce-scatter.15
  1711.4 63.2 reduce-scatter.17
  1777.2 151.8 all-reduce.16
  1932.4 69.1 reduce-scatter.25
  2005.0 67.3 reduce-scatter.19
  2076.0 67.3 reduce-scatter.21
  2146.9 109.6 reduce-scatter.27
  2260.2 109.9 reduce-scatter.29
  2373.8 110.3 reduce-scatter.31
where the time goes:
time: 2510 us; the launch traced here: 2490 us
  waiting for transfers between devices  1320 us (53%)
  matrix products  647 us (26%)
  other arithmetic  210 us (8%)
  blocking collectives  158 us (6%)
  local copies, waits for them, and re-layouts  139 us (6%)
    dot_general x48, matrix products, group_step(): jnp.einsum('hijk,hjk->hij', weighted, key_matrix, precision=highest_preci...  316 us
    psum x1, waiting for transfers between devices, local(): lax.psum(project(hidden_half, down_full).astype(jnp.bfloat16), 'tensor')  153 us
    psum x1, waiting for transfers between devices, local(): attn = lax.psum(project(gated_half, out_full), 'tensor')  128 us
    reduce_scatter x1, waiting for transfers between devices, local(): lax.psum_scatter(grad_down.astype(jnp.bfloat16), 'dp', scatter_dimension=...  112 us
    reduce_scatter x1, waiting for transfers between devices, local(): lax.psum_scatter(grad_up.astype(jnp.bfloat16), 'dp', scatter_dimension=0,...  111 us
    reduce_scatter x1, waiting for transfers between devices, local(): lax.psum_scatter(grad_gate.astype(jnp.bfloat16), 'dp', scatter_dimension=...  94.9 us
    all_gather x1, waiting for transfers between devices, local(): lax.all_gather(gate_proj.astype(half), 'dp', axis=0, tiled=True)  82.9 us
    psum x1, waiting for transfers between devices, local(): lax.psum((against(d_gate_half, gate_full) + against(d_up_half, up_full))....  81.9 us
  transfers between devices with their start and end apart: 22, of which 17 were waited for; matrix products, arithmetic and copies ran while one was open for 18% of the time, Pallas kernels for 0%

commit v1 on v0

--- a/solution.py
+++ b/solution.py
@@ -221,9 +221,12 @@
     d_up_half = d_up.astype(half)
     grad_gate = collect(normed_ffn_half, d_gate_half)
     grad_up = collect(normed_ffn_half, d_up_half)
-    d_normed_ffn = lax.psum(
-        (against(d_gate_half, gate_full) + against(d_up_half, up_full)).astype(jnp.bfloat16),
-        "tensor",
+    d_normed_ffn = jnp.sum(
+        lax.all_gather(
+            (against(d_gate_half, gate_full) + against(d_up_half, up_full)).astype(jnp.bfloat16),
+            "tensor",
+        ),
+        axis=0,
     ).astype(jnp.float32)
     d_middle_norm, grad_gain_ffn = pull_second(d_normed_ffn)
     grad_norm_ffn, grad_gate_proj, grad_up_proj, grad_down_proj = (

time: 2510 us -> 2200 us (0.88)
  waiting for transfers between devices: 1320 us -> 998 us
    reduce_scatter x1, waiting for transfers between devices: 112 us -> 0.01 us  [local(): lax.psum_scatter(grad_down.astype(jnp.bfloat16), 'dp', scatter_dimension=...]
    reduce_scatter x1, waiting for transfers between devices: 111 us -> 0.01 us  [local(): lax.psum_scatter(grad_up.astype(jnp.bfloat16), 'dp', scatter_dimension=0,...]
    reduce_scatter x1, waiting for transfers between devices: 94.9 us -> 0.02 us  [local(): lax.psum_scatter(grad_gate.astype(jnp.bfloat16), 'dp', scatter_dimension=...]
    psum x1 -> x0, waiting for transfers between devices: 81.9 us -> none  [local(): lax.psum((against(d_gate_half, gate_full) + against(d_up_half, up_full))....]
    all_gather x0 -> x1, waiting for transfers between devices: none -> 68.1 us  [local(): lax.all_gather((against(d_gate_half, gate_full) + against(d_up_half, up_f...]
    unnamed x24, waiting for transfers between devices: 24.7 us -> 54.9 us
  transfers between devices with their start and end apart: 22 -> 22, of which waited for: 17 -> 14; matrix products, arithmetic and copies ran while one was open for 18% -> 43% of each run, Pallas kernels for 0% -> 0%
where the time goes in v1:
time: 2200 us; the launch traced here: 2190 us
  waiting for transfers between devices  998 us (45%)
  matrix products  648 us (29%)
  other arithmetic  222 us (10%)
  blocking collectives  159 us (7%)
  local copies, waits for them, and re-layouts  137 us (6%)
    dot_general x48, matrix products, group_step(): jnp.einsum('hijk,hjk->hij', weighted, key_matrix, precision=highest_preci...  317 us
    psum x1, waiting for transfers between devices, local(): lax.psum(project(hidden_half, down_full).astype(jnp.bfloat16), 'tensor')  153 us
    psum x1, waiting for transfers between devices, local(): attn = lax.psum(project(gated_half, out_full), 'tensor')  128 us
    all_gather x1, waiting for transfers between devices, local(): lax.all_gather(gate_proj.astype(half), 'dp', axis=0, tiled=True)  82.9 us
    all_gather x1, waiting for transfers between devices, local(): lax.all_gather(down_proj.astype(half), 'dp', axis=1, tiled=True)  81.7 us
    all_gather x1, waiting for transfers between devices, local(): lax.all_gather(up_proj.astype(half), 'dp', axis=0, tiled=True)  80.7 us
    reduce_scatter x1, waiting for transfers between devices, local(): lax.psum_scatter(grad_value.astype(jnp.bfloat16), 'dp', scatter_dimension...  69.1 us
    dot_general x9, matrix products, against(): lax.dot_general(left, right, (((1,), (1,)), ((), ())), preferred_element_...  68.9 us
  transfers between devices with their start and end apart: 22, of which 14 were waited for; matrix products, arithmetic and copies ran while one was open for 43% of the time, Pallas kernels for 0%

profile of v1, /device:TPU:0, one launch (start us, length us, event | category | flops | bytes accessed | tf_op | source)
XLA Modules:
  0.0 2186.6 jit_solution(9842876419639555176)
XLA Ops:
  19.4 22.3 %all-gather.1 = bf16[8,1,256]{2,1,0:T(2,128)(2,1)S(1)} all-gather(bf16[1,1,256]{2,1,0:T(2,128)(2,1)S(1)} %reshape.739), channel_id=1, replica_groups=mesh['dp'=8,'tensor'=4] {'dp'}, dimensions={0}, use_global_device_ids=true | all-gather | bytes 4608 | tf_op jit(solution)/shard_map/all_gather | solution.py:157
  41.7 30.6 %all_gather.58 = bf16[2048,16]{0,1:T(8,128)(2,1)S(1)} all-gather(bf16[256,16]{0,1:T(8,128)(2,1)S(1)} %convert_element_type.285), channel_id=1, replica_groups=mesh['dp'=8,'tensor'=4] {'dp'}, dimensions={0}, use_global_device_ids=true | all-gather | bytes 73728 | tf_op jit(solution)/shard_map/all_gather | solution.py:162
  74.7 17.5 all-reduce.7
  92.4 30.9 %all_gather.59 = bf16[16,1,256]{0,1,2:T(2,128)(2,1)S(1)} all-gather(bf16[16,1,32]{0,1,2:T(2,128)(2,1)S(1)} %copy.93), channel_id=1, replica_groups=mesh['dp'=8,'tensor'=4] {'dp'}, dimensions={2}, use_global_device_ids=true | all-gather | bytes 9216 | tf_op jit(solution)/shard_map/all_gather | solution.py:163
  153.1 229.4 %while.40 = (s32[]{:T(128)}, f32[1,1,256,512]{3,2,1,0:T(8,128)S(1)}, f32[16,1,1,64,512]{4,3,2,1,0:T(8,128)S(1)}, f32[16,1,1,256,512]{4,3,2,1,0:T(8,128)}, f32[16...) while((s32[]{:T(128)}, ...), condition=%wide.region_3.4_spmd.clone.clone, body=%wide.region_1.3_spmd.clone.sunk.clone | while | flops 245047296 | bytes 12723313 | solution.py:73
  402.8 18.1 all-gather.2
  421.6 127.8 %all-reduce.12.cloned.1.call-done = f32[1024,2048]{1,0:T(8,128)} async-done(((f32[1024,2048]{1,0:T(8,128)}), f32[1024,2048]{1,0:T(8,128)}) %all-reduce.12.cloned.1.call-update) | async-done | bytes 8388624 | tf_op jit(solution)/shard_map/psum | solution.py:191
  561.2 82.9 %all-gather.23.cloned.1.call-done = bf16[2048,1408]{1,0:T(8,128)(2,1)} async-done(((bf16[256,1408]{1,0:T(8,128)(2,1)}), bf16[2048,1408]{1,0:T(8,128)(2,1)}) %all-gather.23.cloned.1.call-update) | async-done | bytes 5767184 | tf_op jit(solution)/shard_map/all_gather | solution.py:195
  656.1 80.7 %all-gather.25.cloned.1.call-done = bf16[2048,1408]{1,0:T(8,128)(2,1)} async-done(((bf16[256,1408]{1,0:T(8,128)(2,1)}), bf16[2048,1408]{1,0:T(8,128)(2,1)}) %all-gather.25.cloned.1.call-update) | async-done | bytes 5767184 | tf_op jit(solution)/shard_map/all_gather | solution.py:196
  748.5 81.7 %all-gather.27.cloned.1.call-done = bf16[1408,2048]{1,0:T(8,128)(2,1)} async-done(((bf16[1408,256]{1,0:T(8,128)(2,1)}), bf16[1408,2048]{1,0:T(8,128)(2,1)}) %all-gather.27.cloned.1.call-update) | async-done | bytes 5767184 | tf_op jit(solution)/shard_map/all_gather | solution.py:197
  830.2 15.8 multiply_convert_fusion.2
  876.6 12.1 convolution_convert_fusion.1
  901.5 68.1 %all-gather.29.cloned.1.call-done = bf16[4096,2048]{1,0:T(8,128)(2,1)} async-done(((bf16[1024,2048]{1,0:T(8,128)(2,1)}), bf16[4096,2048]{1,0:T(8,128)(2,1)}) %all-gather.29.cloned.1.call-update) | async-done | bytes 16777232 | tf_op jit(solution)/shard_map/all_gather | solution.py:225
  969.5 12.1 reduce_sum.158
  1002.5 467.7 %while.41 = (s32[]{:T(128)}, f32[1,1,256,512]{2,3,1,0:T(8,128)S(1)}, f32[16,1,1,64,256]{4,3,2,1,0:T(8,128)S(1)}, bf16[16,1,1,64,256]{4,3,2,1,0:T(8,128)(2,1)}, b...) while((s32[]{:T(128)}, ...), condition=%wide.region_19.20_spmd.clone.clone, body=%wide.region_11.19_spmd.clone.sunk.clone | while | flops 502210560 | bytes 24297648 | solution.py:73
  1564.0 54.2 %reduce-scatter.34.cloned.1.call-done = bf16[32,16]{1,0:T(8,128)(2,1)} async-done(((bf16[256,16]{1,0:T(8,128)(2,1)}), bf16[32,16]{1,0:T(8,128)(2,1)}) %reduce-scatter.34.cloned.1.call-update) | async-done | bytes 1040
  1619.6 56.0 %reduce-scatter.24.cloned.1.call-done = bf16[256,16]{0,1:T(8,128)(2,1)} async-done(((bf16[2048,16]{0,1:T(8,128)(2,1)}), bf16[256,16]{0,1:T(8,128)(2,1)}) %reduce-scatter.24.cloned.1.call-update) | async-done | bytes 8208 | tf_op jit(solution)/shard_map/reduce_scatter | solution.py:325
  1676.9 65.2 %reduce-scatter.16.cloned.1.call-done = bf16[256,256]{1,0:T(8,128)(2,1)} async-done(((bf16[2048,256]{1,0:T(8,128)(2,1)}), bf16[256,256]{1,0:T(8,128)(2,1)}) %reduce-scatter.16.cloned.1.call-update) | async-done | bytes 131088 | tf_op jit(solution)/shard_map/reduce_scatter | solution.py:313
  1743.7 64.8 %reduce-scatter.18.cloned.1.call-done = bf16[256,256]{1,0:T(8,128)(2,1)} async-done(((bf16[2048,256]{1,0:T(8,128)(2,1)}), bf16[256,256]{1,0:T(8,128)(2,1)}) %reduce-scatter.18.cloned.1.call-update) | async-done | bytes 131088 | tf_op jit(solution)/shard_map/reduce_scatter | solution.py:316
  1810.1 153.4 %all-reduce.14.cloned.1.call-done = (bf16[1024,2048]{1,0:T(8,128)(2,1)}, bf16[1024,2048]{1,0:T(8,128)(2,1)}) async-done(((bf16[1024,2048]{1,0:T(8,128)(2,1)}, bf16[1024,2048]{1,0:T(8,128)(2,1)}), (bf16[1024,2048]{1,0:T(8,128)(2,1)}, bf16[1024,2048]{1,0:T(8,128)(2,1)})) %all-reduce.14.cloned.1.call-update) | async-done | bytes 8388624 | tf_op jit(solution)/shard_map/psum | solution.py:205
  1970.7 22.5 %all-reduce.6 = (bf16[2048]{0:T(1024)(128)(2,1)S(1)}, bf16[512]{0:T(512)(128)(2,1)S(1)}, bf16[2048]{0:T(1024)(128)(2,1)S(1)}) all-reduce(bf16[2048]{0:T(1024)(128)(2,1)S(1)} %get-tuple-element.576, bf16[512]{0:T(512)(128)(2,1)S(1)} %get-tuple-element.578, ...), channel_id=3, replica_groups=mesh['dp'=8,'tensor'=4] {'dp'}, use_global_device_ids=true, to_apply=%region_24.25.clone | all-reduce | flops 4608 | bytes 18432
  1999.8 36.1 %reduce-scatter.26.cloned.1.call-done = bf16[512,256]{1,0:T(8,128)(2,1)} async-done(((bf16[512,2048]{1,0:T(8,128)(2,1)}), bf16[512,256]{1,0:T(8,128)(2,1)}) %reduce-scatter.26.cloned.1.call-update) | async-done | bytes 262160 | tf_op jit(solution)/shard_map/reduce_scatter | solution.py:337
  2037.7 69.1 %reduce-scatter.20.cloned.1.call-done = bf16[256,512]{1,0:T(8,128)(2,1)} async-done(((bf16[2048,512]{1,0:T(8,128)(2,1)}), bf16[256,512]{1,0:T(8,128)(2,1)}) %reduce-scatter.20.cloned.1.call-update) | async-done | bytes 262160 | tf_op jit(solution)/shard_map/reduce_scatter | solution.py:319
  2125.0 52.7 %reduce-scatter.22.cloned.1.call-done = bf16[256,512]{1,0:T(8,128)(2,1)} async-done(((bf16[2048,512]{1,0:T(8,128)(2,1)}), bf16[256,512]{1,0:T(8,128)(2,1)}) %reduce-scatter.22.cloned.1.call-update) | async-done | bytes 262160 | tf_op jit(solution)/shard_map/reduce_scatter | solution.py:322
  (933 shorter events, 990.3 us)
Async XLA Ops:
  7.2 125.4 %all-gather.17.cloned.1.call-start = ((), (), s32[]{:S(2)}) async-start(), calls=%async_computation.13 | async-start | bytes 1179648 | tf_op jit(solution)/shard_map/all_gather | solution.py:158
  8.9 128.5 %all-gather.13.cloned.1.call-start = ((), (), s32[]{:S(2)}) async-start(), calls=%async_computation.11 | async-start | bytes 1179648 | tf_op jit(solution)/shard_map/all_gather | solution.py:159
  10.6 135.9 %all-gather.15.cloned.1.call-start = ((), (), s32[]{:S(2)}) async-start(), calls=%async_computation.12 | async-start | bytes 2359296 | tf_op jit(solution)/shard_map/all_gather | solution.py:160
  12.5 370.4 %all-gather.19.cloned.1.call-start = ((), (), s32[]{:S(2)}) async-start(), calls=%async_computation.14 | async-start | bytes 2359296 | tf_op jit(solution)/shard_map/all_gather | solution.py:161
  14.3 376.0 %all-gather.21.cloned.1.call-start = ((), (), s32[]{:S(2)}) async-start(), calls=%async_computation.15 | async-start | bytes 2359296 | tf_op jit(solution)/shard_map/all_gather | solution.py:166
  16.2 533.3 %all-reduce.12.cloned.1.call-start = ((), (), s32[]{:S(2)}) async-start(), calls=%async_computation.16 | async-start | bytes 16777216 | tf_op jit(solution)/shard_map/psum | solution.py:191
  397.9 246.2 %all-gather.23.cloned.1.call-start = ((), (), s32[]{:S(2)}) async-start(), calls=%async_computation.17 | async-start | bytes 6488064 | tf_op jit(solution)/shard_map/all_gather | solution.py:195
  400.2 336.6 %all-gather.25.cloned.1.call-start = ((), (), s32[]{:S(2)}) async-start(), calls=%async_computation.18 | async-start | bytes 6488064 | tf_op jit(solution)/shard_map/all_gather | solution.py:196
  401.2 429.0 %all-gather.27.cloned.1.call-start = ((), (), s32[]{:S(2)}) async-start(), calls=%async_computation.19 | async-start | bytes 6488064 | tf_op jit(solution)/shard_map/all_gather | solution.py:197
  402.7 566.8 %all-gather.29.cloned.1.call-start = ((), (), s32[]{:S(2)}) async-start(), calls=%async_computation.29 | async-start | bytes 20971520 | tf_op jit(solution)/shard_map/all_gather | solution.py:225
  865.3 690.5 %reduce-scatter.28.cloned.1.call-start = ((), (), s32[]{:S(2)}) async-start(), calls=%async_computation.26 | async-start | bytes 6488064 | tf_op jit(solution)/shard_map/reduce_scatter | solution.py:236
  876.5 681.6 %reduce-scatter.30.cloned.1.call-start = ((), (), s32[]{:S(2)}) async-start(), calls=%async_computation.27 | async-start | bytes 6488064 | tf_op jit(solution)/shard_map/reduce_scatter | solution.py:239
  888.7 671.7 %reduce-scatter.32.cloned.1.call-start = ((), (), s32[]{:S(2)}) async-start(), calls=%async_computation.28 | async-start | bytes 6488064 | tf_op jit(solution)/shard_map/reduce_scatter | solution.py:242
  901.4 661.3 %reduce-scatter.36.cloned.1.call-start = ((), (), s32[]{:S(2)}) async-start(), calls=%async_computation.31 | async-start | bytes 73728
  1489.3 128.9 %reduce-scatter.34.cloned.1.call-start = ((), (), s32[]{:S(2)}) async-start(), calls=%async_computation.30 | async-start | bytes 73728
  1490.7 184.9 %reduce-scatter.24.cloned.1.call-start = ((), (), s32[]{:S(2)}) async-start(), calls=%async_computation.24 | async-start | bytes 73728 | tf_op jit(solution)/shard_map/reduce_scatter | solution.py:325
  1491.3 250.8 %reduce-scatter.16.cloned.1.call-start = ((), (), s32[]{:S(2)}) async-start(), calls=%async_computation.20 | async-start | bytes 1179648 | tf_op jit(solution)/shard_map/reduce_scatter | solution.py:313
  1495.9 312.5 %reduce-scatter.18.cloned.1.call-start = ((), (), s32[]{:S(2)}) async-start(), calls=%async_computation.21 | async-start | bytes 1179648 | tf_op jit(solution)/shard_map/reduce_scatter | solution.py:316
  1509.4 454.1 %all-reduce.14.cloned.1.call-start = ((), (), s32[]{:S(2)}) async-start(), calls=%async_computation.32 | async-start | bytes 16777216 | tf_op jit(solution)/shard_map/psum | solution.py:205
  1533.8 502.1 %reduce-scatter.26.cloned.1.call-start = ((), (), s32[]{:S(2)}) async-start(), calls=%async_computation.25 | async-start | bytes 2359296 | tf_op jit(solution)/shard_map/reduce_scatter | solution.py:337
  1542.2 564.7 %reduce-scatter.20.cloned.1.call-start = ((), (), s32[]{:S(2)}) async-start(), calls=%async_computation.22 | async-start | bytes 2359296 | tf_op jit(solution)/shard_map/reduce_scatter | solution.py:319
  1548.1 629.6 %reduce-scatter.22.cloned.1.call-start = ((), (), s32[]{:S(2)}) async-start(), calls=%async_computation.23 | async-start | bytes 2359296 | tf_op jit(solution)/shard_map/reduce_scatter | solution.py:322
  1554.4 409.1 %copy-start.23 = (bf16[2048,16]{0,1:T(8,128)(2,1)S(1)}, bf16[2048,16]{0,1:T(8,128)(2,1)}, u32[]{:S(2)}) copy-start(bf16[2048,16]{0,1:T(8,128)(2,1)} %copy-done.22) | copy-start | bytes 196612
  1554.4 409.1 %copy-start.25 = (f32[8,1,256]{2,1,0:T(1,128)S(1)}, f32[8,1,256]{2,1,0:T(1,128)}, u32[]{:S(2)}) copy-start(f32[8,1,256]{2,1,0:T(1,128)} %copy-done.24) | copy-start | bytes 24580
  (48 other events, 1674.9 us)
Sparse Core Ops, SparseCore 0:
  10.7 43.2 all-gather.16
  56.7 38.8 all-gather.12
  98.3 48.2 all-gather.14
  149.1 47.6 all-gather.18
  199.2 49.1 all-gather.20
  398.0 151.4 all-reduce.11
  551.6 92.4 all-gather.22
  646.3 90.4 all-gather.24
  738.8 91.3 all-gather.26
  865.4 104.0 all-gather.28
  973.2 110.5 reduce-scatter.27
  1087.3 109.9 reduce-scatter.29
  1201.0 110.3 reduce-scatter.31
  1489.4 63.3 reduce-scatter.35
  1556.7 61.4 reduce-scatter.33
  1621.7 53.8 reduce-scatter.23
  1678.8 63.1 reduce-scatter.15
  1745.3 63.0 reduce-scatter.17
  1811.6 151.8 all-reduce.13
  1966.8 69.0 reduce-scatter.25
  2039.5 67.2 reduce-scatter.19
  2110.3 67.3 reduce-scatter.21
